TPU v7x, 128 devices: a whole 4x4x4 slice. The times are simulated.
128 devices in a mesh: row: 8 (over z, core), col: 16 (over x, y).
Axes of the slice: x: 4, y: 4, z: 4, core: 2. Of those that a mesh axis runs over, the one named last changes fastest.
Arguments:
- normed: bfloat16 [8192, 7168], P(None, 'col'), may hold values from -44 to 44
- projection_weight: bfloat16 [7168, 3, 7168], P('col', None, 'row')
- adapter_down_weight: bfloat16 [7168, 16, 32], P(None, 'col'), may hold values from -0.0625 to 0.0625
- adapter_up_weight: bfloat16 [16, 2, 16, 7168], P(None, None, None, 'row'), may hold values from -0.47851562 to 0.47851562
- packed_prompt_length: int32 [64], replicated, may hold values from 64 to 512, as said below
- prompt_adapter_ids: int32 [64], replicated, may hold values from 0 to 63, as said below
- slot_adapter_ids: int32 [16], replicated, may hold values from 0 to 63, as said below
- prompt_page_slots: int32 [64, 4], replicated, may hold values from -1 to 159, as said below
Outputs:
- attended: bfloat16 [8192, 7168], P('col', 'row')
- kv_cache: bfloat16 [160, 128, 2, 7168], P('col', None, None, 'row')
Inputs may be any that keep to these rules, and one draw needn't show every extreme that they name: `packed_prompt_length`: the 64 lengths sum to 8192; one of them is exactly 512 and one exactly 64. `slot_adapter_ids`: distinct adapter ids. `prompt_adapter_ids`: every entry is one of slot_adapter_ids, and every loaded adapter is named by at least one prompt. `prompt_page_slots`: entry [i, j] is -1 where 128 * j >= packed_prompt_length[i]; otherwise it lies among slots 10 * c to 10 * c + 9, where c is the block of 512 packed tokens that holds the page's last token. No slot is named twice.
All inputs are finite; a program needn't handle non-finite values.
Results may differ from a plain program's by a relative error of at most 0.0072.
Values may be sent and summed in bfloat16 or wider, within the bound.
A program may use at most 256 MiB of HBM per device.

v0:
```python
import jax
import jax.numpy as jnp
from jax import lax
from jax.sharding import PartitionSpec as P

HEAD_DIM = 128
PAGE = 128
NEAR = 1
SLOTS_DEV = 10
adapter_scale = 2.0
masked_score = -1e30


def shifted(block, axis, distance):
    devices = range(lax.axis_size(axis))
    route = [(i - distance, i) for i in devices if i - distance in devices]
    return lax.ppermute(block, axis, route)


def start_table(packed_prompt_length):
    prompt_ends = jnp.cumsum(packed_prompt_length)
    return prompt_ends - packed_prompt_length


def slot_table(prompt_adapter_ids, slot_adapter_ids):
    active_slots = slot_adapter_ids.shape[0]
    matched = slot_adapter_ids[None, :] == prompt_adapter_ids[:, None]
    return jnp.sum(
        jnp.where(matched, jnp.arange(active_slots, dtype=jnp.int32)[None, :], 0), axis=1
    )


def token_prompts(positions, prompt_starts):
    inside = (positions[:, None] >= prompt_starts[None, :]).astype(jnp.int32)
    return jnp.sum(inside, axis=1) - 1


def token_slots(prompts, slot_of):
    prompt_count = slot_of.shape[0]
    onehot = prompts[:, None] == jnp.arange(prompt_count, dtype=jnp.int32)[None, :]
    return jnp.sum(jnp.where(onehot, slot_of[None, :], 0), axis=1)


def down_term(row_block, slots_here, down_cols, active_slots):
    combined_output = jnp.dot(row_block, down_cols, preferred_element_type=jnp.float32)
    combined_output = combined_output.reshape(row_block.shape[0], active_slots, -1)
    pick_slot = slots_here[:, None] == jnp.arange(active_slots, dtype=jnp.int32)[None, :]
    return jnp.sum(jnp.where(pick_slot[:, :, None], combined_output, 0.0), axis=1)


def local(
    normed,
    projection_weight,
    adapter_down_weight,
    adapter_up_weight,
    packed_prompt_length,
    prompt_adapter_ids,
    slot_adapter_ids,
    prompt_page_slots,
):
    col_count = lax.axis_size("col")
    row_count = lax.axis_size("row")
    col_index = lax.axis_index("col")
    my_row = lax.axis_index("row")
    tok_all, width_loc = normed.shape
    tok_blk = tok_all // col_count
    head_column_span = projection_weight.shape[2]
    heads_loc = head_column_span // HEAD_DIM
    active_slots = slot_adapter_ids.shape[0]
    adapter_rank_width = adapter_up_weight.shape[2]
    prompt_starts = start_table(packed_prompt_length)
    slot_of = slot_table(prompt_adapter_ids, slot_adapter_ids)
    block_start = col_index * tok_blk
    mine = block_start + jnp.arange(tok_blk, dtype=jnp.int32)
    mine_prompts = token_prompts(mine, prompt_starts)
    mine_slots = token_slots(mine_prompts, slot_of)
    down_weight_slices = lax.all_to_all(
        adapter_down_weight, "col", split_axis=0, concat_axis=1, tiled=True
    )
    down_cols = down_weight_slices.reshape(width_loc, -1)
    own_rows = lax.all_to_all(normed, "col", split_axis=0, concat_axis=1, tiled=True)
    weight_piece = lax.all_gather(projection_weight, "col", axis=0, tiled=True)
    flat_piece = weight_piece.reshape(weight_piece.shape[0], -1)
    projection_total = jnp.dot(own_rows, flat_piece, preferred_element_type=jnp.float32)
    rows_per = tok_all // row_count
    row_first = my_row * rows_per
    row_positions = row_first + jnp.arange(rows_per, dtype=jnp.int32)
    row_slots = token_slots(token_prompts(row_positions, prompt_starts), slot_of)
    row_part = lax.dynamic_slice_in_dim(normed, row_first, rows_per, 0)
    summed = lax.psum(down_term(row_part, row_slots, down_cols, active_slots), "col")
    down_every = lax.all_gather(summed.astype(jnp.bfloat16), "row", axis=0, tiled=True)
    local_down_output = lax.dynamic_slice_in_dim(down_every, block_start, tok_blk, 0)
    pick_half = (mine_slots[:, None] == jnp.arange(active_slots, dtype=jnp.int32)[None, :]).astype(
        jnp.bfloat16
    )

    def reduced_rank_rows(low_part, slot_membership):
        token_spread = (pick_half[:, :, None] * low_part[:, None, :]).reshape(
            tok_blk, active_slots * adapter_rank_width
        )
        up_weight_table = adapter_up_weight[:, slot_membership].reshape(
            active_slots * adapter_rank_width, head_column_span
        )
        return jnp.dot(token_spread, up_weight_table, preferred_element_type=jnp.float32)

    query_token_rows = (
        projection_total[:, :head_column_span]
        + adapter_scale * reduced_rank_rows(local_down_output[:, :adapter_rank_width], 0)
    ).astype(jnp.bfloat16)
    key_rows = projection_total[:, head_column_span : 2 * head_column_span].astype(jnp.bfloat16)
    value_token_rows = (
        projection_total[:, 2 * head_column_span :]
        + adapter_scale * reduced_rank_rows(local_down_output[:, adapter_rank_width:], 1)
    ).astype(jnp.bfloat16)
    own_kv = jnp.stack([key_rows, value_token_rows], axis=1)
    earlier = [shifted(own_kv, "col", 1)]
    window = jnp.concatenate(earlier[::-1] + [own_kv], axis=0)
    window_len = window.shape[0]
    window_pos = block_start - NEAR * tok_blk + jnp.arange(window_len, dtype=jnp.int32)
    window_prompts = token_prompts(window_pos, prompt_starts)
    allowed = (mine_prompts[:, None] == window_prompts[None, :]) & (
        window_pos[None, :] <= mine[:, None]
    )
    query_heads = query_token_rows.reshape(tok_blk, heads_loc, HEAD_DIM)
    key_heads = window[:, 0].reshape(window_len, heads_loc, HEAD_DIM)
    value_heads = window[:, 1].reshape(window_len, heads_loc, HEAD_DIM)
    score_scale = HEAD_DIM ** (-0.5)
    scores = (
        jnp.einsum("qhd,khd->hqk", query_heads, key_heads, preferred_element_type=jnp.float32)
        * score_scale
    )
    limited = jnp.where(allowed[None], scores, masked_score)
    peak_score = jnp.max(limited, axis=2, keepdims=True)
    weight = jnp.where(allowed[None], jnp.exp(scores - peak_score), 0.0)
    denominator = jnp.sum(weight, axis=2)
    mixed_heads = jnp.einsum(
        "hqk,khd->qhd", weight.astype(jnp.bfloat16), value_heads, preferred_element_type=jnp.float32
    )
    attended = (
        (mixed_heads / jnp.transpose(denominator)[:, :, None])
        .reshape(tok_blk, head_column_span)
        .astype(jnp.bfloat16)
    )
    prev_kv = earlier[0]
    page_window = jnp.concatenate(
        [prev_kv, own_kv, jnp.zeros((PAGE, 2, head_column_span), jnp.bfloat16)], axis=0
    )
    max_pages = prompt_page_slots.shape[1]
    lens_rep = jnp.repeat(packed_prompt_length, max_pages)
    starts_rep = jnp.repeat(prompt_starts, max_pages)
    page_index = jnp.tile(jnp.arange(max_pages, dtype=jnp.int32), packed_prompt_length.shape[0])
    page_rows = jnp.clip(lens_rep - PAGE * page_index, 0, PAGE)
    page_first = starts_rep + PAGE * page_index
    my_slots = col_index * SLOTS_DEV + jnp.arange(SLOTS_DEV, dtype=jnp.int32)
    slot_hit = prompt_page_slots.reshape(-1)[None, :] == my_slots[:, None]
    rows_used = jnp.sum(jnp.where(slot_hit, page_rows[None, :], 0), axis=1)
    first_used = jnp.sum(jnp.where(slot_hit, page_first[None, :], 0), axis=1)
    offset = jnp.clip(first_used - (col_index - 1) * tok_blk, 0, 2 * tok_blk)
    page_lines = jnp.arange(PAGE, dtype=jnp.int32)
    pick_rows = (offset[:, None] + page_lines[None, :]).reshape(-1)
    taken_rows = jnp.take(page_window, pick_rows, axis=0).reshape(
        SLOTS_DEV, PAGE, 2, head_column_span
    )
    live_rows = (page_lines[None, :] < rows_used[:, None])[:, :, None, None]
    kv_pages = jnp.where(live_rows, taken_rows, jnp.zeros_like(taken_rows))
    return (attended, kv_pages)


def solution(mesh):
    placed = (
        P(None, "col"),
        P("col", None, "row"),
        P(None, "col", None),
        P(None, None, None, "row"),
        P(),
        P(),
        P(),
        P(),
    )
    return jax.shard_map(
        local,
        mesh=mesh,
        in_specs=placed,
        out_specs=(P("col", "row"), P("col", None, None, "row")),
        check_vma=False,
    )
```

profile of v0, /device:TPU:6, one launch (start us, length us, event | category | flops | bytes accessed | tf_op | source)
XLA Modules:
  0.0 544.9 jit_solution(5829252045479823222)
XLA Ops:
  7.2 0.7 all-gather.2.cloned.1.call-update
  7.9 0.5 broadcast.227
  8.4 1.9 reduce.3
  10.3 0.9 copy.105
  11.3 2.4 reshape.319
  13.7 7.4 %all-to-all-start.1 = ((bf16[16,2,7168]{2,1,0:T(2,128)(2,1)}), bf16[16,2,7168]{2,1,0:T(2,128)(2,1)S(1)}, u32[]{:S(2)}, u32[]{:S(2)}) async-start(bf16[16,2,7168]{2,1,0:T(2,128)(2,1)} %reshape.319), calls=%async_computation.1 | async-start | bytes 917504 | tf_op jit(solution)/shard_map/all_to_all | solution.py:77
  21.1 8.1 %copy.104 = bf16[56,16,8,512]{3,2,0,1:T(8,128)(2,1)} copy(bf16[56,16,8,512]{3,2,1,0:T(8,128)(2,1)} %bitcast.61) | data formatting | bytes 14680064 | tf_op jit(solution)/shard_map/all_to_all | solution.py:81
  29.2 1.7 all-to-all-done.1
  31.0 5.9 %all-to-all-start = ((bf16[16,512,448]{1,2,0:T(8,128)(2,1)}), bf16[16,512,448]{1,2,0:T(8,128)(2,1)}, u32[]{:S(2)}, u32[]{:S(2)}) async-start(bf16[16,512,448]{1,2,0:T(8,128)(2,1)} %bitcast.59), calls=%async_computation | async-start | bytes 14680064 | tf_op jit(solution)/shard_map/all_to_all | solution.py:81
  36.9 0.1 copy.82
  37.0 0.1 reduce-window.9
  37.1 0.1 reduce
  37.5 0.1 select_reduce_fusion.3
  37.6 0.1 convert_reduce_fusion
  37.7 0.1 select_reduce_fusion.2
  38.1 4.2 reshape.320
  42.4 7.0 %copy.84 = bf16[7168,1,32]{0,2,1:T(8,128)(2,1)S(1)} copy(bf16[7168,1,32]{2,1,0:T(2,128)(2,1)} %reshape.320) | data formatting | bytes 917504 | tf_op jit(solution)/shard_map/all_to_all | solution.py:77
  49.4 0.6 all_to_all.30
  50.0 1.9 select_reduce_fusion.1
  52.0 199.3 %all-reduce.1 = bf16[1024,32]{0,1:T(8,128)(2,1)S(1)} all-reduce(f32[1024,32]{0,1:T(8,128)S(1)} %select_reduce_fusion.1), channel_id=1, replica_groups=mesh['row'=8,'col'=16] {'col'}, use_global_device_ids=true, to_apply=%region_7.8 | all-reduce | flops 32768 | bytes 196608 | tf_op jit(solution)/shard_map/psum | solution.py:90
  251.3 13.7 %all_gather.7 = bf16[8192,32]{0,1:T(8,128)(2,1)S(1)} all-gather(bf16[1024,32]{0,1:T(8,128)(2,1)S(1)} %all-reduce.1), channel_id=1, replica_groups=mesh['row'=8,'col'=16] {'row'}, dimensions={0}, use_global_device_ids=true | all-gather | bytes 589824 | tf_op jit(solution)/shard_map/all_gather | solution.py:91
  265.0 66.0 %all-gather.2.cloned.1.call-done = bf16[7168,3,896]{2,0,1:T(8,128)(2,1)} async-done(((bf16[448,3,896]{2,0,1:T(8,128)(2,1)}), bf16[7168,3,896]{2,0,1:T(8,128)(2,1)}) %all-gather.2.cloned.1.call-update) | async-done | bytes 38535184 | tf_op jit(solution)/shard_map/all_gather | solution.py:82
  331.0 51.4 %copy.81 = bf16[7168,3,896]{0,2,1:T(8,128)(2,1)} copy(bf16[7168,3,896]{2,0,1:T(8,128)(2,1)} %all-gather.2.cloned.1.call-done) | data formatting | bytes 77070336 | tf_op jit(solution)/shard_map/all_gather | solution.py:82
  382.4 28.4 %fusion.38 = f32[512,2688]{1,0:T(8,128)} fusion(bf16[512,7168]{0,1:T(8,128)(2,1)} %bitcast.1, bf16[7168,2688]{0,1:T(8,128)(2,1)} %bitcast.58), kind=kOutput, calls=%fused_computation.78 | convolution fusion | flops 19730006016 | bytes 51380224 | tf_op jit(solution)/shard_map/dot_general | solution.py:84
  410.8 1.6 fusion.16
  412.4 2.0 fusion.15
  414.3 1.4 pad_maximum_fusion
  415.8 1.9 collective-permute-start
  417.7 0.1 copy.91
  417.8 0.1 eq.123
  417.9 0.1 add.145
  418.0 0.1 min.20
  418.1 0.2 fusion.24
  418.6 1.3 compare_and_fusion
  419.9 2.0 fusion.10
  421.9 1.5 copy.87
  423.4 41.3 %collective-permute-done = bf16[512,2,896]{2,0,1:T(8,128)(2,1)} collective-permute-done((bf16[512,2,896]{2,0,1:T(8,128)(2,1)}, bf16[512,2,896]{2,0,1:T(8,128)(2,1)}, u32[]{:S(2)}, u32[]{:S(2)}) %collective-permute-start) | collective-permute-done | bytes 1835040 | tf_op jit(solution)/shard_map/ppermute | solution.py:17
  464.7 1.8 maximum_maximum_fusion.1
  466.5 2.1 fusion.35
  468.6 3.8 copy.88
  472.5 3.1 maximum_maximum_fusion
  475.7 15.3 %copy.92 = bf16[1152,2,896]{2,1,0:T(2,128)(2,1)} copy(bf16[1152,2,896]{2,0,1:T(8,128)(2,1)S(1)} %maximum_maximum_fusion) | data formatting | bytes 8257536 | tf_op jit(solution)/shard_map/concatenate | solution.py:145
  490.9 2.4 copy.86
  493.3 12.7 %fusion.37 = (f32[7,512]{1,0:T(8,128)S(1)}, bf16[7,512,1024]{2,1,0:T(8,128)(2,1)}) fusion(pred[512,1024]{1,0:T(8,128)(4,1)S(1)} %copy-done.4, bf16[512,7,128]{0,2,1:T(8,128)(2,1)S(1)} %bitcast.68, bf16[1024,7,128]{0,2,1:T(8,128)(2,1)} %bitcast.62), kind=kOutput, calls=%fused_computation.77 | convolution fusion | flops 1904739328 | bytes 10631168 | tf_op jit(solution)/shard_map/sub | solution.py:134
  506.0 5.7 %fusion.12 = bf16[512,7,128]{0,2,1:T(8,128)(2,1)S(1)} fusion(bf16[1024,7,128]{0,2,1:T(8,128)(2,1)S(1)} %bitcast.63, bf16[7,512,1024]{2,1,0:T(8,128)(2,1)} %get-tuple-element.29, f32[512,7]{0,1:T(8,128)S(1)} %bitcast.72), kind=kOutput, calls=%fused_computation.25 | convolution fusion | flops 940441600 | bytes 10106880 | tf_op jit(solution)/shard_map/hqk,khd->qhd/dot_general | solution.py:136
  511.7 1.3 copy.93
  513.0 16.6 %gather_fusion = bf16[1280,2,896]{2,1,0:T(2,128)(2,1)} fusion(bf16[1152,2,896]{2,1,0:T(2,128)(2,1)} %copy.92, s32[2048]{0:T(1024)S(1)} %pad_clamp_fusion), kind=kCustom, calls=%fused_computation | custom fusion | bytes 9180160 | tf_op jit(solution)/shard_map/jit(_take)/gather | solution.py:161
  529.6 8.5 %broadcast_select_fusion.1 = bf16[10,128,2,896]{3,2,1,0:T(2,128)(2,1)} fusion(pred[10,128]{1,0:T(8,128)(4,1)S(1)} %iota_compare_fusion.4, bf16[10,128,2,896]{3,2,1,0:T(2,128)(2,1)} %bitcast.60, pred[10,128]{1,0:T(8,128)(4,1)S(1)} %fusion.28), kind=kLoop, calls=%fused_computation.7 | loop fusion | flops 4587520 | bytes 9177600 | tf_op jit(solution)/shard_map/jit(_where)/select_n | solution.py:165
  (44 shorter events, 0.9 us)
Async XLA Ops:
  7.2 323.8 %all-gather.2.cloned.1.call-start = ((), (), s32[]{:S(2)}) async-start(), calls=%async_computation.2 | async-start | bytes 40943616 | tf_op jit(solution)/shard_map/all_gather | solution.py:82
  13.7 17.3 %all-to-all-start.1 = ((bf16[16,2,7168]{2,1,0:T(2,128)(2,1)}), bf16[16,2,7168]{2,1,0:T(2,128)(2,1)S(1)}, u32[]{:S(2)}, u32[]{:S(2)}) async-start(bf16[16,2,7168]{2,1,0:T(2,128)(2,1)} %reshape.319), calls=%async_computation.1 | async-start | bytes 917504 | tf_op jit(solution)/shard_map/all_to_all | solution.py:77
  31.0 5.9 %copy-start.5 = (s32[64]{0:T(128)S(1)}, s32[64]{0:T(128)}, u32[]{:S(2)}) copy-start(s32[64]{0:T(128)} %param.12) | copy-start | bytes 772
  31.0 6.3 %copy-start.7 = (s32[64]{0:T(128)S(1)}, s32[64]{0:T(128)}, u32[]{:S(2)}) copy-start(s32[64]{0:T(128)} %param.13) | copy-start | bytes 772
  31.0 6.3 %copy-start.8 = (s32[16]{0:T(128)S(1)}, s32[16]{0:T(128)}, u32[]{:S(2)}) copy-start(s32[16]{0:T(128)} %param.14) | copy-start | bytes 196
  31.0 7.1 %copy-start.2 = (bf16[16,2,16,896]{3,2,1,0:T(8,128)(2,1)S(1)}, bf16[16,2,16,896]{3,2,1,0:T(8,128)(2,1)}, u32[]{:S(2)}) copy-start(bf16[16,2,16,896]{3,2,1,0:T(8,128)(2,1)} %param.11) | copy-start | bytes 2752516
  31.0 351.4 %all-to-all-start = ((bf16[16,512,448]{1,2,0:T(8,128)(2,1)}), bf16[16,512,448]{1,2,0:T(8,128)(2,1)}, u32[]{:S(2)}, u32[]{:S(2)}) async-start(bf16[16,512,448]{1,2,0:T(8,128)(2,1)} %bitcast.59), calls=%async_computation | async-start | bytes 14680064 | tf_op jit(solution)/shard_map/all_to_all | solution.py:81
  410.8 6.9 %copy-start.6 = (s32[64,4]{0,1:T(4,128)S(1)}, s32[64,4]{0,1:T(4,128)}, u32[]{:S(2)}) copy-start(s32[64,4]{0,1:T(4,128)} %param.15) | copy-start | bytes 3076
  415.8 49.0 %collective-permute-start = (bf16[512,2,896]{2,0,1:T(8,128)(2,1)}, bf16[512,2,896]{2,0,1:T(8,128)(2,1)}, u32[]{:S(2)}, u32[]{:S(2)}) collective-permute-start(bf16[512,2,896]{2,0,1:T(8,128)(2,1)} %pad_maximum_fusion), channel_id=1, source_target_pairs={{0,1},{1,2},{2,3},{3,4},{4,5},{5,6},{6,7},{7,8},{8,9},{9,10},{10,1... | collective-permute-start | bytes 5505032 | tf_op jit(solution)/shard_map/ppermute | solution.py:17
  475.6 15.3 %copy-start = (bf16[1024,1,896]{2,0,1:T(8,128)(2,1)S(1)}, bf16[1024,1,896]{2,0,1:T(8,128)(2,1)}, u32[]{:S(2)}) copy-start(bf16[1024,1,896]{2,0,1:T(8,128)(2,1)} %get-tuple-element.21) | copy-start | bytes 5505028
  475.6 17.7 %copy-start.3 = (bf16[512,896]{0,1:T(8,128)(2,1)S(1)}, bf16[512,896]{0,1:T(8,128)(2,1)}, u32[]{:S(2)}) copy-start(bf16[512,896]{0,1:T(8,128)(2,1)} %copy.87) | copy-start | bytes 2752516
  475.6 17.7 %copy-start.4 = (pred[512,1024]{1,0:T(8,128)(4,1)S(1)}, pred[512,1024]{1,0:T(8,128)(4,1)}, u32[]{:S(2)}) copy-start(pred[512,1024]{1,0:T(8,128)(4,1)} %compare_and_fusion) | copy-start | bytes 1572868
  493.3 12.7 %copy-start.1 = (bf16[1024,1,896]{0,2,1:T(8,128)(2,1)S(1)}, bf16[1024,1,896]{0,2,1:T(8,128)(2,1)}, u32[]{:S(2)}) copy-start(bf16[1024,1,896]{0,2,1:T(8,128)(2,1)} %copy.86) | copy-start | bytes 5505028
Sparse Core Ops, SparseCore 0:
  10.1 320.8 all-gather.1
where the time goes:
time: 547 us; the launch traced here: 545 us
  blocking collectives  213 us (39%)
  local copies, waits for them, and re-layouts  120 us (22%)
  waiting for transfers between devices  110 us (20%)
  matrix products  52.6 us (10%)
  other arithmetic  19.5 us (4%)
  starting transfers between devices  15.3 us (3%)
  between operations  14.3 us (3%)
    psum x1, blocking collectives, local(): lax.psum(down_term(row_part, row_slots, down_cols, active_slots), 'col')  199 us
    all_gather x1, waiting for transfers between devices, local(): weight_piece = lax.all_gather(projection_weight, 'col', axis=0, tiled=True)  66 us
    all_gather x1, local copies, waits for them, and re-layouts, local(): weight_piece = lax.all_gather(projection_weight, 'col', axis=0, tiled=True)  51.4 us
    ppermute x1, waiting for transfers between devices, shifted(): return lax.ppermute(block, axis, route)  41.3 us
    dot_general x1, matrix products, local(): jnp.dot(own_rows, flat_piece, preferred_element_type=jnp.float32)  28.4 us
    gather x1, local copies, waits for them, and re-layouts, local(): jnp.take(page_window, pick_rows, axis=0)  16.6 us
    concatenate x2, local copies, waits for them, and re-layouts, local(): jnp.concatenate([prev_kv, own_kv, jnp.zeros((PAGE, 2, head_column_span),...  15.3 us
    all_gather x1, blocking collectives, local(): lax.all_gather(summed.astype(jnp.bfloat16), 'row', axis=0, tiled=True)  13.7 us
  transfers between devices with their start and end apart: 4, of which 3 were waited for; matrix products, arithmetic and copies ran while one was open for 16% of the time, Pallas kernels for 0%

commit v1 on v0

--- a/solution.py
+++ b/solution.py
@@ -87,7 +87,9 @@
     row_positions = row_first + jnp.arange(rows_per, dtype=jnp.int32)
     row_slots = token_slots(token_prompts(row_positions, prompt_starts), slot_of)
     row_part = lax.dynamic_slice_in_dim(normed, row_first, rows_per, 0)
-    summed = lax.psum(down_term(row_part, row_slots, down_cols, active_slots), "col")
+    part = down_term(row_part, row_slots, down_cols, active_slots)
+    terms = lax.all_gather(part, "col", axis=0, tiled=False)
+    summed = terms.sum(axis=0)
     down_every = lax.all_gather(summed.astype(jnp.bfloat16), "row", axis=0, tiled=True)
     local_down_output = lax.dynamic_slice_in_dim(down_every, block_start, tok_blk, 0)
     pick_half = (mine_slots[:, None] == jnp.arange(active_slots, dtype=jnp.int32)[None, :]).astype(

time: 547 us -> 617 us (1.13)
  waiting for transfers between devices: 110 us -> 374 us
  blocking collectives: 213 us -> 15.2 us
    psum x1 -> x0, blocking collectives: 199 us -> none  [local(): lax.psum(down_term(row_part, row_slots, down_cols, active_slots), 'col')]
    all_gather x1, waiting for transfers between devices: 66 us -> 222 us  [local(): weight_piece = lax.all_gather(projection_weight, 'col', axis=0, tiled=True)]
    all_gather x0 -> x1, waiting for transfers between devices: none -> 105 us  [local(): terms = lax.all_gather(part, 'col', axis=0, tiled=False)]
    all_to_all x1, waiting for transfers between devices: 1.74 us -> 7.99 us  [local(): lax.all_to_all(adapter_down_weight, 'col', split_axis=0, concat_axis=1, t...]
  transfers between devices with their start and end apart: 4 -> 5, of which waited for: 3 -> 4; matrix products, arithmetic and copies ran while one was open for 16% -> 11% of each run, Pallas kernels for 0% -> 0%
where the time goes in v1:
time: 617 us; the launch traced here: 615 us
  waiting for transfers between devices  374 us (61%)
  local copies, waits for them, and re-layouts  122 us (20%)
  matrix products  53.3 us (9%)
  other arithmetic  19.8 us (3%)
  starting transfers between devices  16.4 us (3%)
  blocking collectives  15.2 us (2%)
  between operations  14.4 us (2%)
    all_gather x1, waiting for transfers between devices, local(): weight_piece = lax.all_gather(projection_weight, 'col', axis=0, tiled=True)  222 us
    all_gather x1, waiting for transfers between devices, local(): terms = lax.all_gather(part, 'col', axis=0, tiled=False)  105 us
    all_gather x1, local copies, waits for them, and re-layouts, local(): weight_piece = lax.all_gather(projection_weight, 'col', axis=0, tiled=True)  51.5 us
    ppermute x1, waiting for transfers between devices, shifted(): return lax.ppermute(block, axis, route)  38.2 us
    dot_general x1, matrix products, local(): jnp.dot(own_rows, flat_piece, preferred_element_type=jnp.float32)  28.4 us
    gather x1, local copies, waits for them, and re-layouts, local(): jnp.take(page_window, pick_rows, axis=0)  16.6 us
    concatenate x2, local copies, waits for them, and re-layouts, local(): jnp.concatenate([prev_kv, own_kv, jnp.zeros((PAGE, 2, head_column_span),...  15.3 us
    all_gather x1, blocking collectives, local(): lax.all_gather(summed.astype(jnp.bfloat16), 'row', axis=0, tiled=True)  15.2 us
  transfers between devices with their start and end apart: 5, of which 4 were waited for; matrix products, arithmetic and copies ran while one was open for 11% of the time, Pallas kernels for 0%

profile of v1, /device:TPU:6, one launch (start us, length us, event | category | flops | bytes accessed | tf_op | source)
XLA Modules:
  0.0 614.7 jit_solution(6641930894091566892)
XLA Ops:
  7.2 0.5 broadcast.227
  7.7 1.9 reduce.3
  9.6 0.9 copy.106
  10.6 2.4 reshape.320
  13.0 7.4 %all-to-all-start.1 = ((bf16[16,2,7168]{2,1,0:T(2,128)(2,1)}), bf16[16,2,7168]{2,1,0:T(2,128)(2,1)S(1)}, u32[]{:S(2)}, u32[]{:S(2)}) async-start(bf16[16,2,7168]{2,1,0:T(2,128)(2,1)} %reshape.320), calls=%async_computation.1 | async-start | bytes 917504 | tf_op jit(solution)/shard_map/all_to_all | solution.py:77
  20.5 0.1 copy.82
  20.7 0.1 reduce
  20.8 0.1 convert_reduce_fusion
  21.1 0.1 select_reduce_fusion.2
  21.2 8.0 %all-to-all-done.1 = bf16[16,2,7168]{2,1,0:T(2,128)(2,1)S(1)} async-done(((bf16[16,2,7168]{2,1,0:T(2,128)(2,1)}), bf16[16,2,7168]{2,1,0:T(2,128)(2,1)S(1)}, u32[]{:S(2)}, u32[]{:S(2)}) %all-to-all-start.1) | async-done | bytes 458784 | tf_op jit(solution)/shard_map/all_to_all | solution.py:77
  29.2 4.2 reshape.321
  33.5 7.0 %copy.84 = bf16[7168,1,32]{0,2,1:T(8,128)(2,1)S(1)} copy(bf16[7168,1,32]{2,1,0:T(2,128)(2,1)} %reshape.321) | data formatting | bytes 917504 | tf_op jit(solution)/shard_map/all_to_all | solution.py:77
  40.5 0.6 all_to_all.30
  41.1 2.6 select_reduce_fusion.1
  43.8 0.7 all-gather.4.cloned.1.call-update
  44.5 6.8 %copy.105 = bf16[56,16,8,512]{3,2,0,1:T(8,128)(2,1)} copy(bf16[56,16,8,512]{3,2,1,0:T(8,128)(2,1)} %bitcast.66) | data formatting | bytes 14680064 | tf_op jit(solution)/shard_map/all_to_all | solution.py:81
  51.3 6.7 %all-to-all-start = ((bf16[16,512,448]{1,2,0:T(8,128)(2,1)}), bf16[16,512,448]{1,2,0:T(8,128)(2,1)}, u32[]{:S(2)}, u32[]{:S(2)}) async-start(bf16[16,512,448]{1,2,0:T(8,128)(2,1)} %bitcast.64), calls=%async_computation | async-start | bytes 14680064 | tf_op jit(solution)/shard_map/all_to_all | solution.py:81
  58.5 104.7 %all-gather.6.cloned.1.call-done = f32[16384,32]{0,1:T(8,128)} async-done(((f32[1024,32]{0,1:T(8,128)}), f32[16384,32]{0,1:T(8,128)}) %all-gather.6.cloned.1.call-update) | async-done | bytes 2097168 | tf_op jit(solution)/shard_map/all_gather | solution.py:91
  163.2 2.8 copy.97
  166.0 0.3 bitcast_reduce_fusion
  166.3 15.2 %all_gather.15 = bf16[8192,32]{0,1:T(8,128)(2,1)S(1)} all-gather(bf16[1024,32]{0,1:T(8,128)(2,1)S(1)} %bitcast_reduce_fusion), channel_id=1, replica_groups=mesh['row'=8,'col'=16] {'row'}, dimensions={0}, use_global_device_ids=true | all-gather | bytes 589824 | tf_op jit(solution)/shard_map/all_gather | solution.py:93
  181.6 222.0 %all-gather.4.cloned.1.call-done = bf16[7168,3,896]{2,0,1:T(8,128)(2,1)} async-done(((bf16[448,3,896]{2,0,1:T(8,128)(2,1)}), bf16[7168,3,896]{2,0,1:T(8,128)(2,1)}) %all-gather.4.cloned.1.call-update) | async-done | bytes 38535184 | tf_op jit(solution)/shard_map/all_gather | solution.py:82
  403.6 51.5 %copy.81 = bf16[7168,3,896]{0,2,1:T(8,128)(2,1)} copy(bf16[7168,3,896]{2,0,1:T(8,128)(2,1)} %all-gather.4.cloned.1.call-done) | data formatting | bytes 77070336 | tf_op jit(solution)/shard_map/all_gather | solution.py:82
  455.1 28.4 %fusion.38 = f32[512,2688]{1,0:T(8,128)} fusion(bf16[512,7168]{0,1:T(8,128)(2,1)} %bitcast.1, bf16[7168,2688]{0,1:T(8,128)(2,1)} %bitcast.63), kind=kOutput, calls=%fused_computation.79 | convolution fusion | flops 19730006016 | bytes 51380224 | tf_op jit(solution)/shard_map/dot_general | solution.py:84
  483.5 1.6 fusion.16
  485.1 2.0 fusion.15
  487.0 1.4 pad_maximum_fusion
  488.4 2.2 collective-permute-start
  490.7 0.1 copy.91
  490.8 0.1 eq.123
  490.9 0.1 add.143
  491.0 0.1 min.20
  491.1 0.2 fusion.24
  491.6 1.3 compare_and_fusion
  492.9 2.0 fusion.10
  494.8 1.5 copy.87
  496.3 38.2 %collective-permute-done = bf16[512,2,896]{2,0,1:T(8,128)(2,1)} collective-permute-done((bf16[512,2,896]{2,0,1:T(8,128)(2,1)}, bf16[512,2,896]{2,0,1:T(8,128)(2,1)}, u32[]{:S(2)}, u32[]{:S(2)}) %collective-permute-start) | collective-permute-done | bytes 1835040 | tf_op jit(solution)/shard_map/ppermute | solution.py:17
  534.5 1.8 maximum_maximum_fusion.1
  536.3 2.1 fusion.35
  538.5 3.8 copy.88
  542.3 3.1 maximum_maximum_fusion
  545.5 15.3 %copy.92 = bf16[1152,2,896]{2,1,0:T(2,128)(2,1)} copy(bf16[1152,2,896]{2,0,1:T(8,128)(2,1)S(1)} %maximum_maximum_fusion) | data formatting | bytes 8257536 | tf_op jit(solution)/shard_map/concatenate | solution.py:147
  560.8 2.4 copy.86
  563.2 12.7 %fusion.37 = (f32[7,512]{1,0:T(8,128)S(1)}, bf16[7,512,1024]{2,1,0:T(8,128)(2,1)}) fusion(pred[512,1024]{1,0:T(8,128)(4,1)S(1)} %copy-done.4, bf16[512,7,128]{0,2,1:T(8,128)(2,1)S(1)} %bitcast.74, bf16[1024,7,128]{0,2,1:T(8,128)(2,1)} %bitcast.68), kind=kOutput, calls=%fused_computation.78 | convolution fusion | flops 1904739328 | bytes 10631168 | tf_op jit(solution)/shard_map/sub | solution.py:136
  575.9 5.7 fusion.12
  581.5 1.3 copy.93
  582.8 16.6 %gather_fusion = bf16[1280,2,896]{2,1,0:T(2,128)(2,1)} fusion(bf16[1152,2,896]{2,1,0:T(2,128)(2,1)} %copy.92, s32[2048]{0:T(1024)S(1)} %pad_clamp_fusion), kind=kCustom, calls=%fused_computation | custom fusion | bytes 9180160 | tf_op jit(solution)/shard_map/jit(_take)/gather | solution.py:163
  599.4 8.5 %broadcast_select_fusion.1 = bf16[10,128,2,896]{3,2,1,0:T(2,128)(2,1)} fusion(pred[10,128]{1,0:T(8,128)(4,1)S(1)} %iota_compare_fusion.4, bf16[10,128,2,896]{3,2,1,0:T(2,128)(2,1)} %bitcast.65, pred[10,128]{1,0:T(8,128)(4,1)S(1)} %fusion.28), kind=kLoop, calls=%fused_computation.7 | loop fusion | flops 4587520 | bytes 9177600 | tf_op jit(solution)/shard_map/jit(_where)/select_n | solution.py:167
  (48 shorter events, 1.1 us)
Async XLA Ops:
  7.2 13.4 %copy-start.5 = (s32[64]{0:T(128)S(1)}, s32[64]{0:T(128)}, u32[]{:S(2)}) copy-start(s32[64]{0:T(128)} %param.12) | copy-start | bytes 772
  7.2 13.8 %copy-start.8 = (s32[16]{0:T(128)S(1)}, s32[16]{0:T(128)}, u32[]{:S(2)}) copy-start(s32[16]{0:T(128)} %param.14) | copy-start | bytes 196
  7.2 13.8 %copy-start.7 = (s32[64]{0:T(128)S(1)}, s32[64]{0:T(128)}, u32[]{:S(2)}) copy-start(s32[64]{0:T(128)} %param.13) | copy-start | bytes 772
  13.0 16.2 %all-to-all-start.1 = ((bf16[16,2,7168]{2,1,0:T(2,128)(2,1)}), bf16[16,2,7168]{2,1,0:T(2,128)(2,1)S(1)}, u32[]{:S(2)}, u32[]{:S(2)}) async-start(bf16[16,2,7168]{2,1,0:T(2,128)(2,1)} %reshape.320), calls=%async_computation.1 | async-start | bytes 917504 | tf_op jit(solution)/shard_map/all_to_all | solution.py:77
  20.4 142.7 %all-gather.6.cloned.1.call-start = ((), (), s32[]{:S(2)}) async-start(), calls=%async_computation.3 | async-start | bytes 2228224 | tf_op jit(solution)/shard_map/all_gather | solution.py:91
  43.7 359.9 %all-gather.4.cloned.1.call-start = ((), (), s32[]{:S(2)}) async-start(), calls=%async_computation.2 | async-start | bytes 40943616 | tf_op jit(solution)/shard_map/all_gather | solution.py:82
  51.3 7.1 %copy-start.2 = (bf16[16,2,16,896]{3,2,1,0:T(8,128)(2,1)S(1)}, bf16[16,2,16,896]{3,2,1,0:T(8,128)(2,1)}, u32[]{:S(2)}) copy-start(bf16[16,2,16,896]{3,2,1,0:T(8,128)(2,1)} %param.11) | copy-start | bytes 2752516
  51.3 403.8 %all-to-all-start = ((bf16[16,512,448]{1,2,0:T(8,128)(2,1)}), bf16[16,512,448]{1,2,0:T(8,128)(2,1)}, u32[]{:S(2)}, u32[]{:S(2)}) async-start(bf16[16,512,448]{1,2,0:T(8,128)(2,1)} %bitcast.64), calls=%async_computation | async-start | bytes 14680064 | tf_op jit(solution)/shard_map/all_to_all | solution.py:81
  483.5 7.2 %copy-start.6 = (s32[64,4]{0,1:T(4,128)S(1)}, s32[64,4]{0,1:T(4,128)}, u32[]{:S(2)}) copy-start(s32[64,4]{0,1:T(4,128)} %param.15) | copy-start | bytes 3076
  488.4 46.1 %collective-permute-start = (bf16[512,2,896]{2,0,1:T(8,128)(2,1)}, bf16[512,2,896]{2,0,1:T(8,128)(2,1)}, u32[]{:S(2)}, u32[]{:S(2)}) collective-permute-start(bf16[512,2,896]{2,0,1:T(8,128)(2,1)} %pad_maximum_fusion), channel_id=1, source_target_pairs={{0,1},{1,2},{2,3},{3,4},{4,5},{5,6},{6,7},{7,8},{8,9},{9,10},{10,1... | collective-permute-start | bytes 5505032 | tf_op jit(solution)/shard_map/ppermute | solution.py:17
  545.4 15.3 %copy-start = (bf16[1024,1,896]{2,0,1:T(8,128)(2,1)S(1)}, bf16[1024,1,896]{2,0,1:T(8,128)(2,1)}, u32[]{:S(2)}) copy-start(bf16[1024,1,896]{2,0,1:T(8,128)(2,1)} %get-tuple-element.21) | copy-start | bytes 5505028
  545.5 17.7 %copy-start.3 = (bf16[512,896]{0,1:T(8,128)(2,1)S(1)}, bf16[512,896]{0,1:T(8,128)(2,1)}, u32[]{:S(2)}) copy-start(bf16[512,896]{0,1:T(8,128)(2,1)} %copy.87) | copy-start | bytes 2752516
  545.5 17.7 %copy-start.4 = (pred[512,1024]{1,0:T(8,128)(4,1)S(1)}, pred[512,1024]{1,0:T(8,128)(4,1)}, u32[]{:S(2)}) copy-start(pred[512,1024]{1,0:T(8,128)(4,1)} %compare_and_fusion) | copy-start | bytes 1572868
  563.2 12.7 %copy-start.1 = (bf16[1024,1,896]{0,2,1:T(8,128)(2,1)S(1)}, bf16[1024,1,896]{0,2,1:T(8,128)(2,1)}, u32[]{:S(2)}) copy-start(bf16[1024,1,896]{0,2,1:T(8,128)(2,1)} %copy.86) | copy-start | bytes 5505028
Sparse Core Ops, SparseCore 0:
  43.8 119.2 all-gather.5
  165.3 238.2 all-gather.3
